TPU v7x, 256 devices: a whole 4x4x8 slice. The times are simulated.
256 devices in a mesh: rows: 64 (over z, x, core), cols: 4 (over y).
Axes of the slice: x: 4, y: 4, z: 8, core: 2. Of those that a mesh axis runs over, the one named last changes fastest.
Arguments:
- front_rows: bfloat16 [8, 8192, 4096], P(None, 'rows', 'cols'), may hold values from -0.0625 to 0.0625
- heights: int32 [64, 8], P('rows'), may hold values from 1 to 128
- child_rows: bfloat16 [65536, 4096], P('rows', 'cols'), may hold values from -0.0625 to 0.0625
- child_dest: int32 [65536, 1], P('rows'), may hold values from 0 to 63; in each aligned block of 1024 rows (0 to 1023, 1024 to 2047, ...) at most 32 rows name the same one
- child_slot: int32 [65536], P('rows'), may hold values from 0 to 127
- parent_ids: int32 [1024], P('rows'), may hold values from 0 to 7
Outputs:
- r_rows: float32 [8, 128, 4096], P(None, None, ('cols', 'rows'))
Inputs may be any that keep to these rules, and one draw needn't show every extreme that they name: `child_dest`: in the rows of one device, at most 32 child rows name one index of rows.
All inputs are finite; a program needn't handle non-finite values.
Results may differ from a plain program's by a relative error of at most 0.002.
Values may be sent and summed in bfloat16 or wider, within the bound.
No kernel may reach another device: no remote copies, remote signals or barrier semaphores. Data moves between devices by JAX's collectives and lax.ppermute only.
A program may use at most 64 MiB of HBM per device.

v0:
```python
import jax
import jax.numpy as jnp
from jax import lax
from jax.sharding import PartitionSpec as P

NB = 128


def from_root(block, axis, holder):
    block = jnp.where(lax.axis_index(axis) == holder, block, jnp.zeros_like(block))
    return lax.psum(block, axis)


def solve_block(lower, columns):
    return jax.scipy.linalg.solve_triangular(lower, columns, lower=True)


def on_device(front_rows, heights, child_rows, child_dest, child_slot, parent_ids):
    fronts, height_cap, width = front_rows.shape
    peers = lax.axis_size("rows")
    child_count = child_rows.shape[0]
    capacity = max(2, 2 * child_count // peers)
    slots = peers * capacity
    destination = child_dest[:, 0]
    hits = (destination[:, None] == jnp.arange(peers, dtype=jnp.int32)[None, :]).astype(jnp.int32)
    before = jnp.cumsum(hits, axis=0) - hits
    position = jnp.sum(before * hits, axis=1)
    send_index = destination * capacity + position
    block_rows = child_count // parent_ids.shape[0]
    child_front = jnp.repeat(parent_ids, block_rows)
    send_rows = jnp.zeros((slots, width), jnp.bfloat16).at[send_index].set(child_rows)
    send_owner = jnp.zeros((slots,), jnp.int32).at[send_index].set(child_front)
    send_front = send_owner.astype(jnp.bfloat16)
    send_slot = (
        jnp.zeros((slots,), jnp.bfloat16).at[send_index].set(child_slot.astype(jnp.bfloat16))
    )
    live_mask = jnp.arange(height_cap, dtype=jnp.int32)[None, :] < heights[0][:, None]
    own = jnp.where(live_mask[:, :, None], front_rows, jnp.zeros_like(front_rows))
    got_rows, got_front, got_slot = (
        lax.all_to_all(
            send_rows.reshape(peers, capacity, width),
            "rows",
            split_axis=0,
            concat_axis=0,
            tiled=True,
        ),
        lax.all_to_all(
            send_front.reshape(peers, capacity), "rows", split_axis=0, concat_axis=0, tiled=True
        ),
        lax.all_to_all(
            send_slot.reshape(peers, capacity), "rows", split_axis=0, concat_axis=0, tiled=True
        ),
    )
    got_rows = got_rows.reshape(slots, width)
    got_lead = got_rows[:, :NB]
    target = got_front.reshape(-1).astype(jnp.int32) * height_cap + got_slot.reshape(-1).astype(
        jnp.int32
    )
    placing = (jnp.arange(fronts * height_cap, dtype=jnp.int32)[:, None] == target[None, :]).astype(
        jnp.bfloat16
    )
    added = jnp.dot(placing, got_lead, preferred_element_type=jnp.float32)
    panel_local = (
        own[:, :, :NB].reshape(fronts * height_cap, NB).astype(jnp.float32) + added
    ).astype(jnp.bfloat16)
    panel = from_root(panel_local.reshape(fronts, height_cap, NB), "cols", 0)
    selected = jnp.dot(
        placing.T, panel.reshape(fronts * height_cap, NB), preferred_element_type=jnp.float32
    ).astype(jnp.bfloat16)
    which = (
        jnp.arange(fronts, dtype=jnp.int32)[:, None]
        == got_front.reshape(-1).astype(jnp.int32)[None, :]
    ).astype(jnp.bfloat16)
    picked = which[:, :, None] * selected[None, :, :]
    child_cross = jnp.einsum("fsk,sc->fkc", picked, got_rows, preferred_element_type=jnp.float32)
    gram = jnp.einsum("fhk,fhj->fkj", panel, panel, preferred_element_type=jnp.float32)
    share_width = width // peers
    cross = jnp.einsum("fhk,fhc->fkc", panel, own, preferred_element_type=jnp.float32) + child_cross
    cross_total, gram_total = lax.psum((cross, gram), "rows")
    start = lax.axis_index("rows") * share_width
    columns = lax.dynamic_slice_in_dim(cross_total, start, share_width, 2)
    lower = jnp.linalg.cholesky(gram_total)
    return jax.vmap(solve_block)(lower, columns)


def solution(mesh):
    placed = (
        P(None, "rows", "cols"),
        P("rows", None),
        P("rows", "cols"),
        P("rows", None),
        P("rows"),
        P("rows"),
    )
    return jax.shard_map(
        on_device,
        mesh=mesh,
        in_specs=placed,
        out_specs=P(None, None, ("cols", "rows")),
        check_vma=False,
    )
```

profile of v0, /device:TPU:8, one launch (start us, length us, event | category | flops | bytes accessed | tf_op | source)
XLA Modules:
  0.0 623.2 jit_solution(7834299393505477574)
XLA Ops:
  6.5 0.7 fusion.21
  7.2 18.0 %reduce-window.6 = s32[64,8,128]{2,1,0:T(8,128)S(1)} reduce-window(s32[64,8,128]{2,1,0:T(8,128)S(1)} %fusion.21, s32[]{:T(128)} %constant.64.clone.1), window={size=1x1x128 pad=0_0x0_0x127_0}, to_apply=%region_0.0 | reduce-window | flops 8323072 | bytes 524292 | tf_op jit(solution)/shard_map/reduce-window
  25.3 0.1 slice.29
  25.4 0.1 copy.37
  25.6 0.1 copy.38
  25.7 0.1 broadcast_add_fusion
  25.8 0.8 fusion.20
  26.6 0.7 compare_select_fusion
  27.3 0.7 broadcast_in_dim.25
  28.0 0.1 reshape.137
  28.1 4.3 scatter_custom_fusion
  32.4 0.7 all_to_all.20
  33.1 11.9 %all-to-all-start = ((bf16[64,1,32]{2,1,0:T(2,128)(2,1)}), bf16[64,1,32]{2,1,0:T(2,128)(2,1)S(1)}, u32[]{:S(2)}, u32[]{:S(2)}) async-start(bf16[64,1,32]{2,1,0:T(2,128)(2,1)} %all_to_all.20), calls=%async_computation | async-start | bytes 65536 | tf_op jit(solution)/shard_map/all_to_all | solution.py:47
  45.0 0.7 convert_element_type.64
  45.7 7.6 %scatter_custom_fusion.1 = bf16[2048]{0:T(1024)(128)(2,1)S(1)} fusion(s32[1024]{0:T(1024)S(1)} %bitcast.56, bf16[1024]{0:T(1024)(128)(2,1)S(1)} %convert_element_type.64, bf16[]{:T(256)} %constant.65.clone.1), kind=kCustom, calls=%fused_computation.48 | custom fusion | bytes 4098 | tf_op jit(solution)/shard_map/scatter | solution.py:35
  53.3 0.7 all_to_all.21
  54.0 0.6 all-to-all-done
  54.6 9.7 %all-to-all-start.1 = ((bf16[64,1,32]{2,1,0:T(2,128)(2,1)}), bf16[64,1,32]{2,1,0:T(2,128)(2,1)S(1)}, u32[]{:S(2)}, u32[]{:S(2)}) async-start(bf16[64,1,32]{2,1,0:T(2,128)(2,1)} %all_to_all.21), calls=%async_computation.1 | async-start | bytes 65536 | tf_op jit(solution)/shard_map/all_to_all | solution.py:50
  64.3 8.6 %scatter_custom_fusion.2 = bf16[2048,1024]{1,0:T(8,128)(2,1)} fusion(s32[1024]{0:T(1024)S(1)} %bitcast.57, bf16[1024,1024]{1,0:T(8,128)(2,1)} %param.8, bf16[]{:T(256)} %constant.65.clone.1), kind=kCustom, calls=%fused_computation.14 | custom fusion | bytes 4194816 | tf_op jit(solution)/shard_map/scatter | solution.py:31
  72.9 1.0 all-to-all-done.1
  73.9 0.0 copy-start.1
  73.9 9.7 %all-to-all-start.2 = ((bf16[64,32,1024]{2,1,0:T(8,128)(2,1)}), bf16[64,32,1024]{2,1,0:T(8,128)(2,1)}, u32[]{:S(2)}, u32[]{:S(2)}) async-start(bf16[64,32,1024]{2,1,0:T(8,128)(2,1)} %bitcast.46), calls=%async_computation.2 | async-start | bytes 8388608 | tf_op jit(solution)/shard_map/all_to_all | solution.py:40
  83.6 0.0 all-reduce.4.cloned.1.call-start
  83.7 0.0 copy-done.1
  83.7 0.1 iota_compare_fusion.16
  83.8 1.8 broadcast_select_fusion
  85.6 0.1 slice.28
  85.7 0.1 convert_reduce_fusion.1
  85.8 0.1 reshape.131
  85.9 0.1 convert_reduce_fusion
  86.0 0.1 reshape.132
  86.0 93.8 %all-to-all-done.2 = bf16[64,32,1024]{2,1,0:T(8,128)(2,1)} async-done(((bf16[64,32,1024]{2,1,0:T(8,128)(2,1)}), bf16[64,32,1024]{2,1,0:T(8,128)(2,1)}, u32[]{:S(2)}, u32[]{:S(2)}) %all-to-all-start.2) | async-done | bytes 4194336 | tf_op jit(solution)/shard_map/all_to_all | solution.py:40
  179.9 3.4 fusion.13
  183.3 0.0 all-reduce.4.cloned.1.call-update
  183.3 0.0 all-reduce.6.cloned.1.call-start
  183.4 42.1 %all-reduce.4.cloned.1.call-done = bf16[8,128,128]{2,1,0:T(8,128)(2,1)} async-done(((bf16[8,128,128]{2,1,0:T(8,128)(2,1)}), bf16[8,128,128]{2,1,0:T(8,128)(2,1)}) %all-reduce.4.cloned.1.call-update) | async-done | bytes 262160 | tf_op jit(solution)/shard_map/psum | solution.py:11
  225.5 3.3 fusion.6
  228.8 0.0 copy-start
  228.8 7.2 %fusion.2 = f32[8,128,1024]{1,2,0:T(8,128)S(1)} fusion(bf16[2048,1024,1]{1,0,2:T(8,128)(2,1)} %bitcast.15, bf16[2048,128]{1,0:T(8,128)(2,1)S(1)} %fusion.6, bf16[8,2048]{1,0:T(8,128)(2,1)S(1)} %fusion.23), kind=kOutput, calls=%fused_computation.6 | convolution fusion | flops 4297064448 | bytes 8945664 | tf_op jit(solution)/shard_map/fsk,sc->fkc/dot_general | solution.py:75
  236.0 0.0 copy-done
  236.1 1.1 fusion.29
  237.2 2.9 convolution_add_fusion
  240.1 0.0 all-reduce.6.cloned.1.call-update
  240.1 198.9 %all-reduce.6.cloned.1.call-done = (f32[8,128,128]{1,2,0:T(8,128)}, f32[8,128,1024]{1,2,0:T(8,128)}) async-done(((f32[8,128,128]{1,2,0:T(8,128)}, f32[8,128,1024]{1,2,0:T(8,128)}), (f32[8,128,128]{1,2,0:T(8,128)}, f32[8,128,1024]{1,2,0:T(8,128)})) %all-reduce.6.cloned.1.call-update) | async-done | bytes 4718608 | tf_op jit(solution)/shard_map/psum | solution.py:79
  439.1 1.2 copy.43
  440.3 1.1 fusion.17
  441.4 94.0 %custom-call.8 = f32[8,128,128]{2,1,0:T(8,128)S(1)} custom-call(f32[8,128,128]{2,1,0:T(8,128)S(1)} %fusion.17), custom_call_target="Cholesky" | custom-call | tf_op jit(solution)/shard_map/jit(cholesky)/cholesky | solution.py:82
  535.4 0.1 select_reduce_fusion
  535.5 0.1 compare_reduce_fusion
  535.6 0.1 select_bitcast_fusion
  535.7 78.6 %custom-call.9 = f32[8,1,128,128]{2,3,1,0:T(8,128)S(1)} custom-call(f32[8,1,128,128]{3,2,1,0:T(8,128)S(1)} %select_bitcast_fusion), custom_call_target="InvertDiagBlocksLowerTriangular" | custom-call | tf_op jit(solution)/shard_map/vmap(jit(_solve_triangular))/triangular_solve | solution.py:15
  614.3 2.0 fusion.15
  (7 shorter events, 0.1 us)
Async XLA Ops:
  33.1 21.6 %all-to-all-start = ((bf16[64,1,32]{2,1,0:T(2,128)(2,1)}), bf16[64,1,32]{2,1,0:T(2,128)(2,1)S(1)}, u32[]{:S(2)}, u32[]{:S(2)}) async-start(bf16[64,1,32]{2,1,0:T(2,128)(2,1)} %all_to_all.20), calls=%async_computation | async-start | bytes 65536 | tf_op jit(solution)/shard_map/all_to_all | solution.py:47
  54.6 19.2 %all-to-all-start.1 = ((bf16[64,1,32]{2,1,0:T(2,128)(2,1)}), bf16[64,1,32]{2,1,0:T(2,128)(2,1)S(1)}, u32[]{:S(2)}, u32[]{:S(2)}) async-start(bf16[64,1,32]{2,1,0:T(2,128)(2,1)} %all_to_all.21), calls=%async_computation.1 | async-start | bytes 65536 | tf_op jit(solution)/shard_map/all_to_all | solution.py:50
  73.9 9.8 %copy-start.1 = (s32[1,8]{1,0:T(1,128)S(1)}, s32[1,8]{1,0:T(1,128)}, u32[]{:S(2)}) copy-start(s32[1,8]{1,0:T(1,128)} %param.7) | copy-start | bytes 100
  73.9 106.0 %all-to-all-start.2 = ((bf16[64,32,1024]{2,1,0:T(8,128)(2,1)}), bf16[64,32,1024]{2,1,0:T(8,128)(2,1)}, u32[]{:S(2)}, u32[]{:S(2)}) async-start(bf16[64,32,1024]{2,1,0:T(8,128)(2,1)} %bitcast.46), calls=%async_computation.2 | async-start | bytes 8388608 | tf_op jit(solution)/shard_map/all_to_all | solution.py:40
  83.6 141.9 %all-reduce.4.cloned.1.call-start = ((), (), s32[]{:S(2)}) async-start(), calls=%async_computation.3 | async-start | bytes 524288 | tf_op jit(solution)/shard_map/psum | solution.py:11
  183.3 255.8 %all-reduce.6.cloned.1.call-start = ((), (), s32[]{:S(2)}) async-start(), calls=%async_computation.4 | async-start | bytes 9437184 | tf_op jit(solution)/shard_map/psum | solution.py:79
  228.8 7.3 %copy-start = (bf16[8,128,128]{2,1,0:T(8,128)(2,1)S(1)}, bf16[8,128,128]{2,1,0:T(8,128)(2,1)}, u32[]{:S(2)}) copy-start(bf16[8,128,128]{2,1,0:T(8,128)(2,1)} %all-reduce.4.cloned.1.call-done) | copy-start | bytes 786436
Sparse Core Ops, SparseCore 0:
  183.4 42.0 all-reduce.3
  240.2 198.7 all-reduce.5
where the time goes:
time: 624 us; the launch traced here: 623 us
  waiting for transfers between devices  336 us (54%)
  other arithmetic  197 us (32%)
  starting transfers between devices  31.4 us (5%)
  local copies, waits for them, and re-layouts  24.5 us (4%)
  matrix products  20 us (3%)
  between operations  13.6 us (2%)
    psum x1, waiting for transfers between devices, on_device(): cross_total, gram_total = lax.psum((cross, gram), 'rows')  199 us
    another operation x4, other arithmetic, on_device(): lower = jnp.linalg.cholesky(gram_total)  94.2 us
    all_to_all x1, waiting for transfers between devices, on_device(): lax.all_to_all(send_rows.reshape(peers, capacity, width), 'rows', split_a...  93.8 us
    another operation x3, other arithmetic, solve_block(): return jax.scipy.linalg.solve_triangular(lower, columns, lower=True)  78.7 us
    psum x1, waiting for transfers between devices, from_root(): return lax.psum(block, axis)  42.1 us
    another operation x3, other arithmetic  18.2 us
  transfers between devices with their start and end apart: 5, of which 5 were waited for; matrix products, arithmetic and copies ran while one was open for 3% of the time, Pallas kernels for 0%

commit v1 on v0

--- a/solution.py
+++ b/solution.py
@@ -8,7 +8,7 @@
 
 def from_root(block, axis, holder):
     block = jnp.where(lax.axis_index(axis) == holder, block, jnp.zeros_like(block))
-    return lax.psum(block, axis)
+    return jnp.sum(lax.all_gather(block, axis), axis=0)
 
 
 def solve_block(lower, columns):

time: 624 us -> 604 us (0.968)
  waiting for transfers between devices: 336 us -> 316 us
    psum x1 -> x0, waiting for transfers between devices: 42.1 us -> none  [from_root(): return lax.psum(block, axis)]
    all_gather x0 -> x1, waiting for transfers between devices: none -> 21.7 us  [from_root(): return jnp.sum(lax.all_gather(block, axis), axis=0)]
where the time goes in v1:
time: 604 us; the launch traced here: 603 us
  waiting for transfers between devices  316 us (52%)
  other arithmetic  199 us (33%)
  starting transfers between devices  31.4 us (5%)
  local copies, waits for them, and re-layouts  24.5 us (4%)
  matrix products  19 us (3%)
  between operations  13.6 us (2%)
    psum x1, waiting for transfers between devices, on_device(): cross_total, gram_total = lax.psum((cross, gram), 'rows')  199 us
    another operation x4, other arithmetic, on_device(): lower = jnp.linalg.cholesky(gram_total)  94.2 us
    all_to_all x1, waiting for transfers between devices, on_device(): lax.all_to_all(send_rows.reshape(peers, capacity, width), 'rows', split_a...  93.8 us
    another operation x3, other arithmetic, solve_block(): return jax.scipy.linalg.solve_triangular(lower, columns, lower=True)  78.7 us
    all_gather x1, waiting for transfers between devices, from_root(): return jnp.sum(lax.all_gather(block, axis), axis=0)  21.7 us
    another operation x3, other arithmetic  18.2 us
  transfers between devices with their start and end apart: 5, of which 5 were waited for; matrix products, arithmetic and copies ran while one was open for 3% of the time, Pallas kernels for 0%

profile of v1, /device:TPU:8, one launch (start us, length us, event | category | flops | bytes accessed | tf_op | source)
XLA Modules:
  0.0 603.1 jit_solution(8440931441772358067)
XLA Ops:
  6.5 0.7 fusion.21
  7.2 18.0 %reduce-window.6 = s32[64,8,128]{2,1,0:T(8,128)S(1)} reduce-window(s32[64,8,128]{2,1,0:T(8,128)S(1)} %fusion.21, s32[]{:T(128)} %constant.66.clone.1), window={size=1x1x128 pad=0_0x0_0x127_0}, to_apply=%region_0.0 | reduce-window | flops 8323072 | bytes 524292 | tf_op jit(solution)/shard_map/reduce-window
  25.3 0.1 slice.29
  25.4 0.1 copy.37
  25.6 0.1 copy.38
  25.7 0.1 broadcast_add_fusion
  25.8 0.8 fusion.20
  26.6 0.7 compare_select_fusion
  27.3 0.7 broadcast_in_dim.25
  28.0 0.1 reshape.147
  28.1 4.3 scatter_custom_fusion
  32.4 0.7 all_to_all.20
  33.1 11.9 %all-to-all-start = ((bf16[64,1,32]{2,1,0:T(2,128)(2,1)}), bf16[64,1,32]{2,1,0:T(2,128)(2,1)S(1)}, u32[]{:S(2)}, u32[]{:S(2)}) async-start(bf16[64,1,32]{2,1,0:T(2,128)(2,1)} %all_to_all.20), calls=%async_computation | async-start | bytes 65536 | tf_op jit(solution)/shard_map/all_to_all | solution.py:47
  45.0 0.7 convert_element_type.66
  45.7 7.6 %scatter_custom_fusion.1 = bf16[2048]{0:T(1024)(128)(2,1)S(1)} fusion(s32[1024]{0:T(1024)S(1)} %bitcast.56, bf16[1024]{0:T(1024)(128)(2,1)S(1)} %convert_element_type.66, bf16[]{:T(256)} %constant.67.clone.1), kind=kCustom, calls=%fused_computation.48 | custom fusion | bytes 4098 | tf_op jit(solution)/shard_map/scatter | solution.py:35
  53.3 0.7 all_to_all.21
  54.0 0.6 all-to-all-done
  54.6 9.7 %all-to-all-start.1 = ((bf16[64,1,32]{2,1,0:T(2,128)(2,1)}), bf16[64,1,32]{2,1,0:T(2,128)(2,1)S(1)}, u32[]{:S(2)}, u32[]{:S(2)}) async-start(bf16[64,1,32]{2,1,0:T(2,128)(2,1)} %all_to_all.21), calls=%async_computation.1 | async-start | bytes 65536 | tf_op jit(solution)/shard_map/all_to_all | solution.py:50
  64.3 8.6 %scatter_custom_fusion.2 = bf16[2048,1024]{1,0:T(8,128)(2,1)} fusion(s32[1024]{0:T(1024)S(1)} %bitcast.57, bf16[1024,1024]{1,0:T(8,128)(2,1)} %param.8, bf16[]{:T(256)} %constant.67.clone.1), kind=kCustom, calls=%fused_computation.14 | custom fusion | bytes 4194816 | tf_op jit(solution)/shard_map/scatter | solution.py:31
  72.9 1.0 all-to-all-done.1
  73.9 0.0 copy-start
  73.9 9.7 %all-to-all-start.2 = ((bf16[64,32,1024]{2,1,0:T(8,128)(2,1)}), bf16[64,32,1024]{2,1,0:T(8,128)(2,1)}, u32[]{:S(2)}, u32[]{:S(2)}) async-start(bf16[64,32,1024]{2,1,0:T(8,128)(2,1)} %bitcast.46), calls=%async_computation.2 | async-start | bytes 8388608 | tf_op jit(solution)/shard_map/all_to_all | solution.py:40
  83.6 0.0 all-gather.2.cloned.1.call-start
  83.7 0.0 copy-done
  83.7 0.1 iota_compare_fusion.16
  83.8 1.8 broadcast_select_fusion
  85.6 0.1 slice.28
  85.7 0.1 convert_reduce_fusion.1
  85.8 0.1 reshape.141
  85.9 0.1 convert_reduce_fusion
  86.0 0.1 reshape.142
  86.0 93.8 %all-to-all-done.2 = bf16[64,32,1024]{2,1,0:T(8,128)(2,1)} async-done(((bf16[64,32,1024]{2,1,0:T(8,128)(2,1)}), bf16[64,32,1024]{2,1,0:T(8,128)(2,1)}, u32[]{:S(2)}, u32[]{:S(2)}) %all-to-all-start.2) | async-done | bytes 4194336 | tf_op jit(solution)/shard_map/all_to_all | solution.py:40
  179.9 3.4 fusion.13
  183.3 0.0 all-gather.2.cloned.1.call-update
  183.3 0.0 all-reduce.3.cloned.1.call-start
  183.4 21.7 %all-gather.2.cloned.1.call-done = bf16[4,8,128,128]{3,2,1,0:T(8,128)(2,1)} async-done(((bf16[1,8,128,128]{3,2,1,0:T(8,128)(2,1)}), bf16[4,8,128,128]{3,2,1,0:T(8,128)(2,1)}) %all-gather.2.cloned.1.call-update) | async-done | bytes 1048592 | tf_op jit(solution)/shard_map/all_gather | solution.py:11
  205.1 1.4 reduce_sum.25
  206.5 1.1 fusion.29
  207.6 2.4 fusion.6
  210.0 7.2 %fusion.2 = f32[8,128,1024]{1,2,0:T(8,128)S(1)} fusion(bf16[2048,1024,1]{1,0,2:T(8,128)(2,1)} %bitcast.15, bf16[2048,128]{1,0:T(8,128)(2,1)S(1)} %fusion.6, bf16[8,2048]{1,0:T(8,128)(2,1)S(1)} %fusion.23), kind=kOutput, calls=%fused_computation.6 | convolution fusion | flops 4297064448 | bytes 8945664 | tf_op jit(solution)/shard_map/fsk,sc->fkc/dot_general | solution.py:75
  217.2 2.9 convolution_add_fusion
  220.1 0.0 all-reduce.3.cloned.1.call-update
  220.2 198.8 %all-reduce.3.cloned.1.call-done = (f32[8,128,128]{1,2,0:T(8,128)}, f32[8,128,1024]{1,2,0:T(8,128)}) async-done(((f32[8,128,128]{1,2,0:T(8,128)}, f32[8,128,1024]{1,2,0:T(8,128)}), (f32[8,128,128]{1,2,0:T(8,128)}, f32[8,128,1024]{1,2,0:T(8,128)})) %all-reduce.3.cloned.1.call-update) | async-done | bytes 4718608 | tf_op jit(solution)/shard_map/psum | solution.py:79
  419.0 1.2 copy.43
  420.2 1.1 fusion.17
  421.3 94.0 %custom-call.8 = f32[8,128,128]{2,1,0:T(8,128)S(1)} custom-call(f32[8,128,128]{2,1,0:T(8,128)S(1)} %fusion.17), custom_call_target="Cholesky" | custom-call | tf_op jit(solution)/shard_map/jit(cholesky)/cholesky | solution.py:82
  515.3 0.1 select_reduce_fusion
  515.4 0.1 compare_reduce_fusion
  515.5 0.1 select_bitcast_fusion
  515.6 78.6 %custom-call.9 = f32[8,1,128,128]{2,3,1,0:T(8,128)S(1)} custom-call(f32[8,1,128,128]{3,2,1,0:T(8,128)S(1)} %select_bitcast_fusion), custom_call_target="InvertDiagBlocksLowerTriangular" | custom-call | tf_op jit(solution)/shard_map/vmap(jit(_solve_triangular))/triangular_solve | solution.py:15
  594.2 2.0 fusion.15
  (7 shorter events, 0.1 us)
Async XLA Ops:
  33.1 21.6 %all-to-all-start = ((bf16[64,1,32]{2,1,0:T(2,128)(2,1)}), bf16[64,1,32]{2,1,0:T(2,128)(2,1)S(1)}, u32[]{:S(2)}, u32[]{:S(2)}) async-start(bf16[64,1,32]{2,1,0:T(2,128)(2,1)} %all_to_all.20), calls=%async_computation | async-start | bytes 65536 | tf_op jit(solution)/shard_map/all_to_all | solution.py:47
  54.6 19.2 %all-to-all-start.1 = ((bf16[64,1,32]{2,1,0:T(2,128)(2,1)}), bf16[64,1,32]{2,1,0:T(2,128)(2,1)S(1)}, u32[]{:S(2)}, u32[]{:S(2)}) async-start(bf16[64,1,32]{2,1,0:T(2,128)(2,1)} %all_to_all.21), calls=%async_computation.1 | async-start | bytes 65536 | tf_op jit(solution)/shard_map/all_to_all | solution.py:50
  73.9 9.8 %copy-start = (s32[1,8]{1,0:T(1,128)S(1)}, s32[1,8]{1,0:T(1,128)}, u32[]{:S(2)}) copy-start(s32[1,8]{1,0:T(1,128)} %param.7) | copy-start | bytes 100
  73.9 106.0 %all-to-all-start.2 = ((bf16[64,32,1024]{2,1,0:T(8,128)(2,1)}), bf16[64,32,1024]{2,1,0:T(8,128)(2,1)}, u32[]{:S(2)}, u32[]{:S(2)}) async-start(bf16[64,32,1024]{2,1,0:T(8,128)(2,1)} %bitcast.46), calls=%async_computation.2 | async-start | bytes 8388608 | tf_op jit(solution)/shard_map/all_to_all | solution.py:40
  83.6 121.5 %all-gather.2.cloned.1.call-start = ((), (), s32[]{:S(2)}) async-start(), calls=%async_computation.3 | async-start | bytes 1310720 | tf_op jit(solution)/shard_map/all_gather | solution.py:11
  183.3 235.7 %all-reduce.3.cloned.1.call-start = ((), (), s32[]{:S(2)}) async-start(), calls=%async_computation.4 | async-start | bytes 9437184 | tf_op jit(solution)/shard_map/psum | solution.py:79
Sparse Core Ops, SparseCore 0:
  183.4 21.6 all-gather.1
  220.2 198.7 all-reduce.2
